TPU v7x, 256 devices: a whole 4x4x8 slice. The times are simulated.
256 devices in a mesh: seq: 32 (over x, z), head: 8 (over y, core).
Axes of the slice: x: 4, y: 4, z: 8, core: 2. Of those that a mesh axis runs over, the one named last changes fastest.
Arguments:
- queries: bfloat16 [32768, 5120], P('seq', 'head')
- keys: bfloat16 [32768, 5120], P('seq', 'head')
- values: bfloat16 [32768, 5120], P('seq', 'head'), may hold values from -6 to 6
- query_gain: float32 [5120], P('head'), may hold values from 0.1 to 1.9
- key_gain: float32 [5120], P('head'), may hold values from 0.1 to 1.9
- shapes: int32 [8, 3], replicated, may hold values from 4 to 32, as said below
- windows: int32 [256, 27], P('seq'), may hold values from -1 to 255, as said below
- text_keys: bfloat16 [32, 256, 5120], P(None, 'seq', 'head')
- text_values: bfloat16 [32, 256, 5120], P(None, 'seq', 'head'), may hold values from -6 to 6
- owner: int32 [8], replicated, may hold values from 0 to 31, as said below
Outputs:
- attended: bfloat16 [32768, 5120], P('seq', 'head')
Inputs may be any that keep to these rules, and one draw needn't show every extreme that they name: `shapes`: row s is (frames, height, width) of video s in tokens: height and width are 16 and 32, or 32 and 16, so a frame has 4 tiles; each video has from 16 to 48 tiles, and the videos' tiles add up to 256, so no tile holds tokens of two videos. `windows`: entry k of row g stands for the tile k // 9 - 1 frames, (k // 3) % 3 - 1 tile rows and k % 3 - 1 tile columns away from tile g in its video: it holds that tile's number or -1; it is -1 wherever that tile lies outside the video, and entry 13 is always g. `owner`: no two videos share a panel.
All inputs are finite; a program needn't handle non-finite values.
Results may differ from a plain program's by a relative error of at most 0.012.
Values may be sent and summed in bfloat16 or wider, within the bound.
A program may use at most 128 MiB of HBM per device.

v0:
```python
import jax
import jax.numpy as jnp
from jax import lax
from jax.sharding import PartitionSpec as P

HEAD_DIM = 128
D = 5120
TILE_H = 8
TILE_W = 16
REACH = 7
TXT = 256
epsilon = 1e-06


def extended_2(cells, sides, width):
    for axis, dim in sides:
        count = lax.axis_size(axis)
        ends = count - 1
        head = lax.slice_in_dim(cells, 0, width, axis=dim)
        tail = lax.slice_in_dim(cells, cells.shape[dim] - width, cells.shape[dim], axis=dim)
        cells = jnp.concatenate(
            [
                lax.ppermute(tail, axis, [(i, (i + 1) % count) for i in range(ends)]),
                cells,
                lax.ppermute(head, axis, [((i + 1) % count, i) for i in range(ends)]),
            ],
            axis=dim,
        )
    return cells


def tile_table(shape_rows):
    per_frame = shape_rows[:, 1] // TILE_H * (shape_rows[:, 2] // TILE_W)
    tile_counts = shape_rows[:, 0] * per_frame
    tile_ends = jnp.cumsum(tile_counts)
    return (tile_ends - tile_counts, tile_ends)


def locate(tile_ids, shape_rows, tile_starts, tile_ends):
    sample_ids = jnp.sum((tile_ids[:, None] >= tile_ends[None, :]).astype(jnp.int32), axis=1)
    one_hot = (
        sample_ids[:, None] == jnp.arange(tile_ends.shape[0], dtype=jnp.int32)[None, :]
    ).astype(jnp.int32)
    first_tiles = jnp.sum(one_hot * tile_starts[None, :], axis=1)
    row_counts = jnp.sum(one_hot * (shape_rows[:, 1] // TILE_H)[None, :], axis=1)
    col_counts = jnp.sum(one_hot * (shape_rows[:, 2] // TILE_W)[None, :], axis=1)
    offsets = tile_ids - first_tiles
    per_frame = row_counts * col_counts
    within = offsets % per_frame
    return (sample_ids, one_hot, offsets // per_frame, within // col_counts, within % col_counts)


def rope_angles(frames, bands, columns, head_size):
    inner = jnp.arange(TILE_H * TILE_W, dtype=jnp.int32)
    tile_total = frames.shape[0]
    time_pos = (
        jnp.broadcast_to(frames[:, None], (tile_total, inner.shape[0]))
        .reshape(-1)
        .astype(jnp.float32)
    )
    row_pos = (bands[:, None] * TILE_H + inner[None, :] // TILE_W).reshape(-1).astype(jnp.float32)
    col_pos = (columns[:, None] * TILE_W + inner[None, :] % TILE_W).reshape(-1).astype(jnp.float32)
    third = head_size // 6
    part_sizes = (head_size - 4 * third, 2 * third, 2 * third)
    angle_parts = []
    for position, part_size in zip((time_pos, row_pos, col_pos), part_sizes):
        frequency = 10000.0 ** (-jnp.arange(0, part_size, 2, dtype=jnp.float32) / part_size)
        angle_parts.append(position[:, None] * frequency[None, :])
    return jnp.concatenate(angle_parts, axis=1)


def rotate(field, angles):
    paired = field.reshape(field.shape[0], field.shape[1], field.shape[2] // 2, 2)
    cosine = jnp.cos(angles)[:, None, :]
    sine = jnp.sin(angles)[:, None, :]
    even_part = paired[..., 0]
    odd_part = paired[..., 1]
    turned = jnp.stack(
        [even_part * cosine - odd_part * sine, even_part * sine + odd_part * cosine], axis=-1
    )
    return turned.reshape(field.shape)


def finish_rows(widened, squares, gain, angles, head_count):
    scaled = widened * lax.rsqrt(squares / D + epsilon)[:, None] * gain[None, :]
    turned = rotate(scaled.reshape(widened.shape[0], head_count, HEAD_DIM), angles)
    return turned.reshape(widened.shape).astype(jnp.bfloat16)


def local(
    queries, keys, values, query_gain, key_gain, shapes, windows, text_keys, text_values, owner
):
    row_count, feat_width = queries.shape
    head_count = feat_width // HEAD_DIM
    tile_rows = TILE_H * TILE_W
    tiles_here = row_count // tile_rows
    first_global = lax.axis_index("seq") * tiles_here
    tile_starts, tile_ends = tile_table(shapes)
    tile_ids = first_global + jnp.arange(tiles_here, dtype=jnp.int32)
    sample_ids, one_hot, frames, bands, columns = locate(tile_ids, shapes, tile_starts, tile_ends)
    angles = rope_angles(frames, bands, columns, HEAD_DIM)
    query_wide = queries.astype(jnp.float32)
    key_wide = keys.astype(jnp.float32)
    query_squares, key_squares = lax.psum(
        (jnp.sum(query_wide * query_wide, axis=1), jnp.sum(key_wide * key_wide, axis=1)), "head"
    )
    q_hat = finish_rows(query_wide, query_squares, query_gain, angles, head_count)
    k_hat = finish_rows(key_wide, key_squares, key_gain, angles, head_count)
    key_value = jnp.stack([k_hat, values])
    extended = extended_2(key_value, (("seq", 1),), REACH * tile_rows)
    panel_of_tile = jnp.sum(one_hot * owner[None, :], axis=1)
    prompt_pair = jnp.stack([text_keys, text_values])
    every_panel = lax.all_gather(prompt_pair, "seq", axis=2, tiled=True)
    wanted = jnp.stack([panel_of_tile[0], panel_of_tile[tiles_here - 1]])
    panels = jnp.take(every_panel, wanted, axis=1)
    prompt_keys = panels[0].reshape(2 * TXT, head_count, HEAD_DIM)
    prompt_values = panels[1].reshape(2 * TXT, head_count, HEAD_DIM)
    second_slot = (sample_ids != sample_ids[0]).astype(jnp.int32)
    prompt_allowed = second_slot[:, None] == (jnp.arange(2 * TXT, dtype=jnp.int32) // TXT)[None, :]
    key_tiles = first_global - REACH + jnp.arange(tiles_here + 2 * REACH, dtype=jnp.int32)
    window_allowed = (
        jnp.any(windows[:, :, None] == key_tiles[None, None, :], axis=1) & (key_tiles >= 0)[None, :]
    )
    group_tiles = 4
    span_tiles = group_tiles + 2 * REACH
    group_rows = group_tiles * tile_rows
    factor = HEAD_DIM ** (-0.5)

    def attend(block_index):
        start_tile = block_index * group_tiles
        query_rows = lax.dynamic_slice_in_dim(q_hat, start_tile * tile_rows, group_rows, 0).reshape(
            group_rows, head_count, HEAD_DIM
        )
        key_rows = lax.dynamic_slice_in_dim(
            extended[0], start_tile * tile_rows, span_tiles * tile_rows, 0
        ).reshape(span_tiles * tile_rows, head_count, HEAD_DIM)
        value_rows = lax.dynamic_slice_in_dim(
            extended[1], start_tile * tile_rows, span_tiles * tile_rows, 0
        ).reshape(span_tiles * tile_rows, head_count, HEAD_DIM)
        allowed = lax.dynamic_slice(
            window_allowed, (start_tile, start_tile), (group_tiles, span_tiles)
        )
        prompt_ok = lax.dynamic_slice_in_dim(prompt_allowed, start_tile, group_tiles, 0)
        key_mask = jnp.concatenate(
            [
                jnp.repeat(jnp.repeat(allowed, tile_rows, axis=0), tile_rows, axis=1),
                jnp.repeat(prompt_ok, tile_rows, axis=0),
            ],
            axis=1,
        )
        all_keys = jnp.concatenate([key_rows, prompt_keys], axis=0)
        all_values = jnp.concatenate([value_rows, prompt_values], axis=0)
        scores = (
            jnp.einsum("qhd,khd->hqk", query_rows, all_keys, preferred_element_type=jnp.float32)
            * factor
        )
        scores = jnp.where(key_mask[None, :, :], scores, -jnp.inf)
        largest = jnp.max(scores, axis=-1, keepdims=True)
        weights = jnp.exp(scores - largest)
        totals = jnp.sum(weights, axis=-1)
        mixed = jnp.einsum(
            "hqk,khd->qhd",
            weights.astype(jnp.bfloat16),
            all_values,
            preferred_element_type=jnp.float32,
        )
        mixed = mixed / jnp.transpose(totals)[:, :, None]
        return mixed.astype(jnp.bfloat16).reshape(group_rows, feat_width)

    outputs = lax.map(attend, jnp.arange(tiles_here // group_tiles, dtype=jnp.int32))
    return outputs.reshape(row_count, feat_width)


def solution(mesh):
    placed = (
        P("seq", "head"),
        P("seq", "head"),
        P("seq", "head"),
        P("head"),
        P("head"),
        P(),
        P("seq", None),
        P(None, "seq", "head"),
        P(None, "seq", "head"),
        P(),
    )
    return jax.shard_map(
        local, mesh=mesh, in_specs=placed, out_specs=P("seq", "head"), check_vma=False
    )
```

profile of v0, /device:TPU:1, one launch (start us, length us, event | category | flops | bytes accessed | tf_op | source)
XLA Modules:
  0.0 366.4 jit_solution(5512880522823748688)
XLA Ops:
  6.5 2.1 pad_maximum_fusion.4
  9.4 15.2 %all-reduce = (f32[1024]{0:T(1024)S(1)}, f32[1024]{0:T(1024)S(1)}) all-reduce(f32[1024]{0:T(1024)S(1)} %fusion.26, f32[1024]{0:T(1024)S(1)} %fusion.28), channel_id=1, replica_groups=mesh['seq'=32,'head'=8] {'head'}, use_global_device_ids=true, to_apply=%region_8.9 | all-reduce | flops 2048 | bytes 16384 | tf_op jit(solution)/shard_map/psum | solution.py:104
  26.3 2.1 copy.28
  28.4 4.5 %reshape_reshape.8 = f32[1024,5,64,2]{0,3,2,1:T(2,128)} reshape(f32[1024,640]{0,1:T(8,128)} %copy.28) | data formatting | bytes 5242880 | tf_op jit(solution)/shard_map/reshape;reshape | solution.py:73
  34.6 2.1 copy.31
  36.7 4.6 %reshape_reshape.9 = f32[1024,5,64,2]{0,3,2,1:T(2,128)} reshape(f32[1024,640]{0,1:T(8,128)} %copy.31) | data formatting | bytes 5242880 | tf_op jit(solution)/shard_map/reshape;reshape | solution.py:73
  43.7 9.1 %subtract_convert_fusion = (bf16[1024,5,64,1]{0,3,2,1:T(2,128)(2,1)}, bf16[1024,5,64,1]{0,3,2,1:T(2,128)(2,1)}, bf16[1024,5,64,1]{0,3,2,1:T(2,128)(2,1)S(1)}, bf16[1024,5,64,1]{0,3,2,1:T(2,128)(2,1)S(1)}) fusion(f32[1024,5,64,2]{0,3,2,1:T(2,128)} %reshape_reshape.9, f32[1024,64]{0,1:T(8,128)S(1)} %get-tuple-element.183, ...), kind=kLoop, calls=%fused_computation.46 | loop fusion | flops 5242880 | bytes 8388608 | tf_op jit(solution)/shard_map/convert.2
  52.8 3.0 pad_maximum_fusion.2
  58.0 2.4 fusion.30
  60.4 3.5 collective-permute-start
  65.3 5.8 %pad_maximum_fusion.3 = bf16[1024,5,64,2]{0,3,2,1:T(2,128)(2,1)} fusion(bf16[1024,5,64,1]{0,3,2,1:T(2,128)(2,1)} %get-tuple-element.173, bf16[1024,5,64,1]{0,3,2,1:T(2,128)(2,1)} %get-tuple-element.172), kind=kLoop, calls=%fused_computation.43 | loop fusion | flops 2621440 | bytes 2621440 | tf_op jit(solution)/shard_map/stack | solution.py:78
  71.1 4.1 %convert_element_type.86 = bf16[1024,640]{0,1:T(8,128)(2,1)} reshape(bf16[1024,5,64,2]{0,3,2,1:T(2,128)(2,1)} %pad_maximum_fusion.3) | data formatting | bytes 2621440 | tf_op jit(solution)/shard_map/convert_element_type | solution.py:87
  79.3 69.1 %collective-permute-done = bf16[2,896,640]{1,2,0:T(8,128)(2,1)} collective-permute-done((bf16[2,896,640]{1,2,0:T(8,128)(2,1)}, bf16[2,896,640]{1,2,0:T(8,128)(2,1)}, u32[]{:S(2)}, u32[]{:S(2)}) %collective-permute-start) | collective-permute-done | bytes 2293792 | tf_op jit(solution)/shard_map/ppermute | solution.py:23
  148.4 10.5 %collective-permute-done.1 = bf16[2,896,640]{1,2,0:T(8,128)(2,1)} collective-permute-done((bf16[2,896,640]{1,2,0:T(8,128)(2,1)}, bf16[2,896,640]{1,2,0:T(8,128)(2,1)}, u32[]{:S(2)}, u32[]{:S(2)}) %collective-permute-start.1) | collective-permute-done | bytes 2293792 | tf_op jit(solution)/shard_map/ppermute | solution.py:25
  158.9 5.7 %pad_maximum_fusion = bf16[2,2816,640]{1,2,0:T(8,128)(2,1)} fusion(bf16[2,896,640]{1,2,0:T(8,128)(2,1)} %collective-permute-done.1, bf16[1,1024,640]{1,2,0:T(8,128)(2,1)S(1)} %bitcast.119, bf16[1,1024,640]{1,2,0:T(8,128)(2,1)S(1)} %convert_element_type.83, bf16[2,896,640]{1,2,0:T(8,128)(2,1)} %collective-permute-done), kind=kLoop, calls=%fused_computation.29 | loop fusion | flops 28835840 | bytes 14417920 | tf_op jit(solution)/shard_map/concatenate | solution.py:21
  164.7 57.8 %all-gather.2.cloned.1.call-done = bf16[2,32,256,640]{3,2,1,0:T(8,128)(2,1)} async-done(((bf16[2,32,8,640]{3,2,1,0:T(8,128)(2,1)}), bf16[2,32,256,640]{3,2,1,0:T(8,128)(2,1)}) %all-gather.2.cloned.1.call-update) | async-done | bytes 20971536 | tf_op jit(solution)/shard_map/all_gather | solution.py:113
  222.5 7.7 %gather_fusion = bf16[2,2,256,640]{3,2,1,0:T(8,128)(2,1)S(1)} fusion(bf16[2,32,256,640]{3,2,1,0:T(8,128)(2,1)} %all-gather.2.cloned.1.call-done, s32[1024]{0:T(1024)S(1)} %pad_clamp_fusion), kind=kCustom, calls=%fused_computation | custom fusion | bytes 2621448 | tf_op jit(solution)/shard_map/jit(_take)/gather | solution.py:115
  234.4 125.1 %while.12 = (s32[]{:T(128)}, bf16[2,512,640]{2,1,0:T(8,128)(2,1)}, bf16[2,2816,640]{1,2,0:T(8,128)(2,1)}, s32[2]{0:T(128)S(1)}, bf16[512,5,128]{0,2,1:T(8,128)(2...) while((s32[]{:T(128)}, bf16[2,512,640]{2,1,0:T(8,128)(2,1)}, ...), condition=%wide.region_14.15_spmd, body=%wide.region_11.14_spmd.sunk | while | flops 3786796032 | bytes 151642208 | solution.py:170
  238.7 3.2 copy.51
  242.7 3.6 fusion.54
  246.3 2.0 constant_dynamic-slice_fusion.9
  248.3 3.3 copy.52
  252.8 15.2 %fusion.55 = (f32[5,512]{1,0:T(8,128)S(1)}, f32[5,512,2816]{2,1,0:T(8,128)}) fusion(pred[512,2816]{1,0:T(8,128)(4,1)} %copy.51, bf16[512,5,128]{0,2,1:T(8,128)(2,1)S(1)} %bitcast.117, bf16[512,5,128]{2,0,1:T(8,128)(2,1)} %get-tuple-element.304, bf16[2304,5,128]{2,0,1:T(8,128)(2,1)} %copy.52), kind=kOutput, calls=%fused_computation.3.clone.1 | convolution fusion | flops 1874327040 | bytes 34547712 | tf_op jit(solution)/shard_map/while/body/eval_jaxpr/qhd,khd->hqk/dot_general | solution.py:154
  268.0 13.8 %fusion.56 = f32[5,512]{1,0:T(8,128)S(1)} fusion(f32[5,512,2816]{2,1,0:T(8,128)} %get-tuple-element.257, f32[5,512]{1,0:T(8,128)S(1)} %get-tuple-element.258, pred[512,2816]{1,0:T(8,128)(4,1)S(1)} %copy-done), kind=kLoop, calls=%fused_computation.4.clone.1 | loop fusion | flops 28833280 | bytes 30298112 | tf_op jit(solution)/shard_map/while/body/eval_jaxpr/reduce_sum | solution.py:160
  281.7 14.1 %divide_convert_fusion.2 = bf16[512,5,128]{0,2,1:T(8,128)(2,1)S(1)} fusion(f32[512,5]{0,1:T(8,128)S(1)} %bitcast.122, f32[5,512,2816]{2,1,0:T(8,128)} %get-tuple-element.257, f32[5,512]{1,0:T(8,128)S(1)} %get-tuple-element.258, pred[512,2816]{1,0:T(8,128)(4,1)S(1)} %copy-done, bf16[512,5,128]{0,2,1:T(8,128)(2,1)S(1)} %copy-done.4, ...), kind=kOutput, calls=%fused_computation.17.clone.1 | convolution fusion | flops 1882193920 | bytes 34557952 | tf_op jit(solution)/shard_map/while/body/eval_jaxpr/hqk,khd->qhd/dot_general | solution.py:161
  301.3 3.2 copy.51
  305.2 3.6 fusion.54
  308.8 2.0 constant_dynamic-slice_fusion.9
  310.9 3.3 copy.52
  315.3 15.2 %fusion.55 = (f32[5,512]{1,0:T(8,128)S(1)}, f32[5,512,2816]{2,1,0:T(8,128)}) fusion(pred[512,2816]{1,0:T(8,128)(4,1)} %copy.51, bf16[512,5,128]{0,2,1:T(8,128)(2,1)S(1)} %bitcast.117, bf16[512,5,128]{2,0,1:T(8,128)(2,1)} %get-tuple-element.304, bf16[2304,5,128]{2,0,1:T(8,128)(2,1)} %copy.52), kind=kOutput, calls=%fused_computation.3.clone.1 | convolution fusion | flops 1874327040 | bytes 34547712 | tf_op jit(solution)/shard_map/while/body/eval_jaxpr/qhd,khd->hqk/dot_general | solution.py:154
  330.5 13.8 %fusion.56 = f32[5,512]{1,0:T(8,128)S(1)} fusion(f32[5,512,2816]{2,1,0:T(8,128)} %get-tuple-element.257, f32[5,512]{1,0:T(8,128)S(1)} %get-tuple-element.258, pred[512,2816]{1,0:T(8,128)(4,1)S(1)} %copy-done), kind=kLoop, calls=%fused_computation.4.clone.1 | loop fusion | flops 28833280 | bytes 30298112 | tf_op jit(solution)/shard_map/while/body/eval_jaxpr/reduce_sum | solution.py:160
  344.3 14.1 %divide_convert_fusion.2 = bf16[512,5,128]{0,2,1:T(8,128)(2,1)S(1)} fusion(f32[512,5]{0,1:T(8,128)S(1)} %bitcast.122, f32[5,512,2816]{2,1,0:T(8,128)} %get-tuple-element.257, f32[5,512]{1,0:T(8,128)S(1)} %get-tuple-element.258, pred[512,2816]{1,0:T(8,128)(4,1)S(1)} %copy-done, bf16[512,5,128]{0,2,1:T(8,128)(2,1)S(1)} %copy-done.4, ...), kind=kOutput, calls=%fused_computation.17.clone.1 | convolution fusion | flops 1882193920 | bytes 34557952 | tf_op jit(solution)/shard_map/while/body/eval_jaxpr/hqk,khd->qhd/dot_general | solution.py:161
  (96 shorter events, 30.0 us)
Async XLA Ops:
  6.5 2.2 copy-start.2
  6.5 2.5 copy-start.3
  6.5 18.1 %copy-start.7 = (f32[640]{0:T(1024)S(1)}, f32[640]{0:T(1024)}, u32[]{:S(2)}) copy-start(f32[640]{0:T(1024)} %param.16) | copy-start | bytes 7684
  6.5 215.9 %all-gather.2.cloned.1.call-start = ((), (), s32[]{:S(2)}) async-start(), calls=%async_computation | async-start | bytes 21626880 | tf_op jit(solution)/shard_map/all_gather | solution.py:113
  28.4 4.5 %copy-start.8 = (f32[640]{0:T(1024)S(1)}, f32[640]{0:T(1024)}, u32[]{:S(2)}) copy-start(f32[640]{0:T(1024)} %param.15) | copy-start | bytes 7684
  36.7 4.6 %copy-start.5 = (s32[8,3]{0,1:T(4,128)S(1)}, s32[8,3]{0,1:T(4,128)}, u32[]{:S(2)}) copy-start(s32[8,3]{0,1:T(4,128)} %param.17) | copy-start | bytes 292
  36.7 5.0 %copy-start.9 = (s32[8]{0:T(128)S(1)}, s32[8]{0:T(128)}, u32[]{:S(2)}) copy-start(s32[8]{0:T(128)} %param.21) | copy-start | bytes 100
  36.7 7.0 %copy-start.1 = (f32[1024,5,64,2]{0,3,2,1:T(2,128)S(1)}, f32[1024,5,64,2]{0,3,2,1:T(2,128)}, u32[]{:S(2)}) copy-start(f32[1024,5,64,2]{0,3,2,1:T(2,128)} %reshape_reshape.8) | copy-start | bytes 7864324
  60.4 88.1 %collective-permute-start = (bf16[2,896,640]{1,2,0:T(8,128)(2,1)}, bf16[2,896,640]{1,2,0:T(8,128)(2,1)}, u32[]{:S(2)}, u32[]{:S(2)}) collective-permute-start(bf16[2,896,640]{1,2,0:T(8,128)(2,1)} %get-tuple-element.176), channel_id=1, source_target_pairs={{0,8},{8,16},{16,24},{24,32},{32,40},{40,48},{48,56},{56,64},{64,7... | collective-permute-start | bytes 6881288 | tf_op jit(solution)/shard_map/ppermute | solution.py:23
  63.8 95.1 %collective-permute-start.1 = (bf16[2,896,640]{1,2,0:T(8,128)(2,1)}, bf16[2,896,640]{1,2,0:T(8,128)(2,1)}, u32[]{:S(2)}, u32[]{:S(2)}) collective-permute-start(bf16[2,896,640]{1,2,0:T(8,128)(2,1)} %get-tuple-element.177), channel_id=1, source_target_pairs={{8,0},{16,8},{24,16},{32,24},{40,32},{48,40},{56,48},{64,56},{72,6... | collective-permute-start | bytes 6881288 | tf_op jit(solution)/shard_map/ppermute | solution.py:25
  65.3 13.2 %copy-start.6 = (s32[8,27]{1,0:T(8,128)S(1)}, s32[8,27]{1,0:T(8,128)}, u32[]{:S(2)}) copy-start(s32[8,27]{1,0:T(8,128)} %param.18) | copy-start | bytes 2596
  252.8 15.2 %copy-start = (pred[512,2816]{1,0:T(8,128)(4,1)S(1)}, pred[512,2816]{1,0:T(8,128)(4,1)}, u32[]{:S(2)}) copy-start(pred[512,2816]{1,0:T(8,128)(4,1)} %copy.51) | copy-start | bytes 4325380 | tf_op jit(solution)/shard_map/while
  268.0 13.8 %copy-start.4 = (bf16[512,5,128]{0,2,1:T(8,128)(2,1)S(1)}, bf16[512,5,128]{0,2,1:T(8,128)(2,1)}, u32[]{:S(2)}) copy-start(bf16[512,5,128]{0,2,1:T(8,128)(2,1)} %get-tuple-element.300) | copy-start | bytes 1966084 | tf_op jit(solution)/shard_map/while
  315.3 15.2 %copy-start = (pred[512,2816]{1,0:T(8,128)(4,1)S(1)}, pred[512,2816]{1,0:T(8,128)(4,1)}, u32[]{:S(2)}) copy-start(pred[512,2816]{1,0:T(8,128)(4,1)} %copy.51) | copy-start | bytes 4325380 | tf_op jit(solution)/shard_map/while
  330.5 13.8 %copy-start.4 = (bf16[512,5,128]{0,2,1:T(8,128)(2,1)S(1)}, bf16[512,5,128]{0,2,1:T(8,128)(2,1)}, u32[]{:S(2)}) copy-start(bf16[512,5,128]{0,2,1:T(8,128)(2,1)} %get-tuple-element.300) | copy-start | bytes 1966084 | tf_op jit(solution)/shard_map/while
Sparse Core Ops, SparseCore 0:
  10.0 212.3 all-gather.1
where the time goes:
time: 367 us; the launch traced here: 366 us
  waiting for transfers between devices  137 us (37%)
  local copies, waits for them, and re-layouts  67.2 us (18%)
  other arithmetic  66.6 us (18%)
  matrix products  58.5 us (16%)
  blocking collectives  15.2 us (4%)
  between operations  13.6 us (4%)
  starting transfers between devices  4.92 us (1%)
    ppermute x1, waiting for transfers between devices, extended_2(): lax.ppermute(tail, axis, [(i, (i + 1) % count) for i in range(ends)])  69.1 us
    all_gather x1, waiting for transfers between devices, local(): every_panel = lax.all_gather(prompt_pair, 'seq', axis=2, tiled=True)  57.8 us
    dot_general x2, matrix products, attend(): jnp.einsum('qhd,khd->hqk', query_rows, all_keys, preferred_element_type=j...  30.4 us
    dot_general x2, matrix products, attend(): jnp.einsum('hqk,khd->qhd', weights.astype(jnp.bfloat16), all_values, pref...  28.1 us
    reduce_sum x2, other arithmetic, attend(): totals = jnp.sum(weights, axis=-1)  27.5 us
    psum x1, blocking collectives, local(): lax.psum((jnp.sum(query_wide * query_wide, axis=1), jnp.sum(key_wide * ke...  15.2 us
    ppermute x1, waiting for transfers between devices, extended_2(): lax.ppermute(head, axis, [((i + 1) % count, i) for i in range(ends)])  10.5 us
    another operation x2, other arithmetic  9.31 us
  transfers between devices with their start and end apart: 3, of which 3 were waited for; matrix products, arithmetic and copies ran while one was open for 15% of the time, Pallas kernels for 0%

commit v1 on v0

--- a/solution.py
+++ b/solution.py
@@ -110,7 +110,9 @@
     extended = extended_2(key_value, (("seq", 1),), REACH * tile_rows)
     panel_of_tile = jnp.sum(one_hot * owner[None, :], axis=1)
     prompt_pair = jnp.stack([text_keys, text_values])
-    every_panel = lax.all_gather(prompt_pair, "seq", axis=2, tiled=True)
+    every_panel = jnp.concatenate(
+        lax.all_to_all(jnp.stack([prompt_pair for _ in range(lax.psum(1, "seq"))]), "seq", 0, 0), 2
+    )
     wanted = jnp.stack([panel_of_tile[0], panel_of_tile[tiles_here - 1]])
     panels = jnp.take(every_panel, wanted, axis=1)
     prompt_keys = panels[0].reshape(2 * TXT, head_count, HEAD_DIM)

time: 367 us -> 741 us (2.02)
  the two profiles are of different devices: /device:TPU:1 before, /device:TPU:103 now
where the time goes in v1:
time: 741 us; the launch traced here: 740 us
  waiting for transfers between devices  489 us (66%)
  local copies, waits for them, and re-layouts  94.4 us (13%)
  other arithmetic  65.3 us (9%)
  matrix products  57.4 us (8%)
  starting transfers between devices  16.4 us (2%)
  blocking collectives  13.8 us (2%)
    ppermute x1, waiting for transfers between devices, extended_2(): lax.ppermute(tail, axis, [(i, (i + 1) % count) for i in range(ends)])  489 us
    dot_general x2, matrix products, attend(): jnp.einsum('qhd,khd->hqk', query_rows, all_keys, preferred_element_type=j...  29.4 us
    dot_general x2, matrix products, attend(): jnp.einsum('hqk,khd->qhd', weights.astype(jnp.bfloat16), all_values, pref...  28.1 us
    reduce_sum x2, other arithmetic, attend(): totals = jnp.sum(weights, axis=-1)  27.5 us
    all_to_all x1, local copies, waits for them, and re-layouts, local(): lax.all_to_all(jnp.stack([prompt_pair for _ in range(lax.psum(1, 'seq'))]...  19.4 us
  transfers between devices with their start and end apart: 3, of which 1 were waited for; matrix products, arithmetic and copies ran while one was open for 8% of the time, Pallas kernels for 0%

profile of v1, /device:TPU:103, one launch (start us, length us, event | category | flops | bytes accessed | tf_op | source)
XLA Modules:
  0.0 739.5 jit_solution(1515073427101441310)
XLA Ops:
  1.1 7.9 %stack.33 = bf16[32,2,32,8,640]{4,3,2,1,0:T(8,128)(2,1)} broadcast(bf16[2,32,8,640]{3,2,1,0:T(8,128)(2,1)S(1)} %pad_maximum_fusion.4), dimensions={1,2,3,4} | broadcast | bytes 21626880 | tf_op jit(solution)/shard_map/stack | solution.py:114
  9.1 10.0 %all-to-all-start = ((bf16[32,2,32,8,640]{4,3,2,1,0:T(8,128)(2,1)}), bf16[32,2,32,8,640]{4,3,2,1,0:T(8,128)(2,1)}, u32[]{:S(2)}, u32[]{:S(2)}) async-start(bf16[32,2,32,8,640]{4,3,2,1,0:T(8,128)(2,1)} %stack.33), calls=%async_computation | async-start | bytes 41943040 | tf_op jit(solution)/shard_map/all_to_all | solution.py:114
  19.8 13.8 %all-reduce = (f32[1024]{0:T(1024)S(1)}, f32[1024]{0:T(1024)S(1)}) all-reduce(f32[1024]{0:T(1024)S(1)} %fusion.26, f32[1024]{0:T(1024)S(1)} %fusion.28), channel_id=1, replica_groups=mesh['seq'=32,'head'=8] {'head'}, use_global_device_ids=true, to_apply=%region_8.9 | all-reduce | flops 2048 | bytes 16384 | tf_op jit(solution)/shard_map/psum | solution.py:104
  35.3 2.1 copy.48
  37.4 4.4 reshape_reshape.8
  43.5 2.1 copy.52
  45.6 4.6 reshape_reshape.9
  52.5 9.1 %subtract_convert_fusion = (bf16[1024,5,64,1]{0,3,2,1:T(2,128)(2,1)}, bf16[1024,5,64,1]{0,3,2,1:T(2,128)(2,1)}, bf16[1024,5,64,1]{0,3,2,1:T(2,128)(2,1)S(1)}, bf16[1024,5,64,1]{0,3,2,1:T(2,128)(2,1)S(1)}) fusion(f32[1024,5,64,2]{0,3,2,1:T(2,128)} %reshape_reshape.9, f32[1024,64]{0,1:T(8,128)S(1)} %get-tuple-element.201, ...), kind=kLoop, calls=%fused_computation.47 | loop fusion | flops 5242880 | bytes 8388608 | tf_op jit(solution)/shard_map/convert.2
  61.7 3.0 pad_maximum_fusion.2
  66.8 2.4 fusion.30
  69.2 4.3 collective-permute-start
  73.5 2.1 collective-permute-start.1
  75.7 5.8 pad_maximum_fusion.3
  81.4 4.1 convert_element_type.86
  89.4 488.9 %collective-permute-done = bf16[2,896,640]{1,2,0:T(8,128)(2,1)} collective-permute-done((bf16[2,896,640]{1,2,0:T(8,128)(2,1)}, bf16[2,896,640]{1,2,0:T(8,128)(2,1)}, u32[]{:S(2)}, u32[]{:S(2)}) %collective-permute-start) | collective-permute-done | bytes 2293792 | tf_op jit(solution)/shard_map/ppermute | solution.py:23
  578.3 5.7 pad_maximum_fusion
  584.0 19.4 %copy.66 = bf16[32,2,32,8,640]{4,3,0,2,1:T(8,128)(2,1)} copy(bf16[32,2,32,8,640]{4,3,2,1,0:T(8,128)(2,1)} %all-to-all-done) | data formatting | bytes 41943040 | tf_op jit(solution)/shard_map/all_to_all | solution.py:114
  603.4 7.7 %gather_fusion = bf16[2,2,256,640]{3,2,1,0:T(8,128)(2,1)S(1)} fusion(bf16[2,32,256,640]{3,2,1,0:T(8,128)(2,1)} %bitcast.121, s32[1024]{0:T(1024)S(1)} %pad_clamp_fusion), kind=kCustom, calls=%fused_computation | custom fusion | bytes 2621448 | tf_op jit(solution)/shard_map/jit(_take)/gather | solution.py:117
  615.4 124.1 %while.12 = (s32[]{:T(128)}, bf16[2,512,640]{2,1,0:T(8,128)(2,1)}, bf16[2,2816,640]{1,2,0:T(8,128)(2,1)}, s32[2]{0:T(128)S(1)}, bf16[512,5,128]{0,2,1:T(8,128)(2...) while((s32[]{:T(128)}, bf16[2,512,640]{2,1,0:T(8,128)(2,1)}, ...), condition=%wide.region_14.15_spmd, body=%wide.region_11.14_spmd.sunk | while | flops 3786796032 | bytes 151642208 | solution.py:172
  619.7 3.2 copy.74
  623.6 3.6 fusion.54
  627.2 2.1 constant_dynamic-slice_fusion.9
  629.3 3.3 copy.75
  633.8 14.7 %fusion.55 = (f32[5,512]{1,0:T(8,128)S(1)}, f32[5,512,2816]{2,1,0:T(8,128)}) fusion(pred[512,2816]{1,0:T(8,128)(4,1)} %copy.74, bf16[512,5,128]{0,2,1:T(8,128)(2,1)S(1)} %bitcast.123, bf16[512,5,128]{2,0,1:T(8,128)(2,1)} %get-tuple-element.322, bf16[2304,5,128]{2,0,1:T(8,128)(2,1)} %copy.75), kind=kOutput, calls=%fused_computation.3.clone.1 | convolution fusion | flops 1874327040 | bytes 34547712 | tf_op jit(solution)/shard_map/while/body/eval_jaxpr/qhd,khd->hqk/dot_general | solution.py:156
  648.5 13.8 %fusion.56 = f32[5,512]{1,0:T(8,128)S(1)} fusion(f32[5,512,2816]{2,1,0:T(8,128)} %get-tuple-element.275, f32[5,512]{1,0:T(8,128)S(1)} %get-tuple-element.276, pred[512,2816]{1,0:T(8,128)(4,1)S(1)} %copy-done), kind=kLoop, calls=%fused_computation.4.clone.1 | loop fusion | flops 28833280 | bytes 30298112 | tf_op jit(solution)/shard_map/while/body/eval_jaxpr/reduce_sum | solution.py:162
  662.2 14.0 %divide_convert_fusion.2 = bf16[512,5,128]{0,2,1:T(8,128)(2,1)S(1)} fusion(f32[512,5]{0,1:T(8,128)S(1)} %bitcast.128, f32[5,512,2816]{2,1,0:T(8,128)} %get-tuple-element.275, f32[5,512]{1,0:T(8,128)S(1)} %get-tuple-element.276, pred[512,2816]{1,0:T(8,128)(4,1)S(1)} %copy-done, bf16[512,5,128]{0,2,1:T(8,128)(2,1)S(1)} %copy-done.4, ...), kind=kOutput, calls=%fused_computation.17.clone.1 | convolution fusion | flops 1882193920 | bytes 34557952 | tf_op jit(solution)/shard_map/while/body/eval_jaxpr/hqk,khd->qhd/dot_general | solution.py:163
  681.8 3.2 copy.74
  685.7 3.6 fusion.54
  691.4 3.3 copy.75
  695.8 14.7 %fusion.55 = (f32[5,512]{1,0:T(8,128)S(1)}, f32[5,512,2816]{2,1,0:T(8,128)}) fusion(pred[512,2816]{1,0:T(8,128)(4,1)} %copy.74, bf16[512,5,128]{0,2,1:T(8,128)(2,1)S(1)} %bitcast.123, bf16[512,5,128]{2,0,1:T(8,128)(2,1)} %get-tuple-element.322, bf16[2304,5,128]{2,0,1:T(8,128)(2,1)} %copy.75), kind=kOutput, calls=%fused_computation.3.clone.1 | convolution fusion | flops 1874327040 | bytes 34547712 | tf_op jit(solution)/shard_map/while/body/eval_jaxpr/qhd,khd->hqk/dot_general | solution.py:156
  710.5 13.8 %fusion.56 = f32[5,512]{1,0:T(8,128)S(1)} fusion(f32[5,512,2816]{2,1,0:T(8,128)} %get-tuple-element.275, f32[5,512]{1,0:T(8,128)S(1)} %get-tuple-element.276, pred[512,2816]{1,0:T(8,128)(4,1)S(1)} %copy-done), kind=kLoop, calls=%fused_computation.4.clone.1 | loop fusion | flops 28833280 | bytes 30298112 | tf_op jit(solution)/shard_map/while/body/eval_jaxpr/reduce_sum | solution.py:162
  724.3 14.0 %divide_convert_fusion.2 = bf16[512,5,128]{0,2,1:T(8,128)(2,1)S(1)} fusion(f32[512,5]{0,1:T(8,128)S(1)} %bitcast.128, f32[5,512,2816]{2,1,0:T(8,128)} %get-tuple-element.275, f32[5,512]{1,0:T(8,128)S(1)} %get-tuple-element.276, pred[512,2816]{1,0:T(8,128)(4,1)S(1)} %copy-done, bf16[512,5,128]{0,2,1:T(8,128)(2,1)S(1)} %copy-done.4, ...), kind=kOutput, calls=%fused_computation.17.clone.1 | convolution fusion | flops 1882193920 | bytes 34557952 | tf_op jit(solution)/shard_map/while/body/eval_jaxpr/hqk,khd->qhd/dot_general | solution.py:163
  (97 shorter events, 31.4 us)
Async XLA Ops:
  9.1 10.0 %copy-start.2 = (bf16[1024,640]{1,0:T(8,128)(2,1)S(1)}, bf16[1024,640]{1,0:T(8,128)(2,1)}, u32[]{:S(2)}) copy-start(bf16[1024,640]{1,0:T(8,128)(2,1)} %param.13) | copy-start | bytes 3932164
  9.1 10.4 %copy-start.3 = (bf16[1024,640]{1,0:T(8,128)(2,1)S(1)}, bf16[1024,640]{1,0:T(8,128)(2,1)}, u32[]{:S(2)}) copy-start(bf16[1024,640]{1,0:T(8,128)(2,1)} %param.12) | copy-start | bytes 3932164
  9.1 575.0 %all-to-all-start = ((bf16[32,2,32,8,640]{4,3,2,1,0:T(8,128)(2,1)}), bf16[32,2,32,8,640]{4,3,2,1,0:T(8,128)(2,1)}, u32[]{:S(2)}, u32[]{:S(2)}) async-start(bf16[32,2,32,8,640]{4,3,2,1,0:T(8,128)(2,1)} %stack.33), calls=%async_computation | async-start | bytes 41943040 | tf_op jit(solution)/shard_map/all_to_all | solution.py:114
  19.1 14.5 %copy-start.7 = (f32[640]{0:T(1024)S(1)}, f32[640]{0:T(1024)}, u32[]{:S(2)}) copy-start(f32[640]{0:T(1024)} %param.16) | copy-start | bytes 7684
  37.4 4.5 copy-start.8
  45.6 4.6 copy-start.5
  45.6 5.0 copy-start.9
  45.6 7.0 copy-start.1
  69.2 509.1 %collective-permute-start = (bf16[2,896,640]{1,2,0:T(8,128)(2,1)}, bf16[2,896,640]{1,2,0:T(8,128)(2,1)}, u32[]{:S(2)}, u32[]{:S(2)}) collective-permute-start(bf16[2,896,640]{1,2,0:T(8,128)(2,1)} %get-tuple-element.194), channel_id=1, source_target_pairs={{0,8},{8,16},{16,24},{24,32},{32,40},{40,48},{48,56},{56,64},{64,7... | collective-permute-start | bytes 6881288 | tf_op jit(solution)/shard_map/ppermute | solution.py:23
  73.5 504.8 %collective-permute-start.1 = (bf16[2,896,640]{1,2,0:T(8,128)(2,1)}, bf16[2,896,640]{1,2,0:T(8,128)(2,1)}, u32[]{:S(2)}, u32[]{:S(2)}) collective-permute-start(bf16[2,896,640]{1,2,0:T(8,128)(2,1)} %get-tuple-element.195), channel_id=1, source_target_pairs={{8,0},{16,8},{24,16},{32,24},{40,32},{48,40},{56,48},{64,56},{72,6... | collective-permute-start | bytes 6881288 | tf_op jit(solution)/shard_map/ppermute | solution.py:25
  75.6 12.9 %copy-start.6 = (s32[8,27]{1,0:T(8,128)S(1)}, s32[8,27]{1,0:T(8,128)}, u32[]{:S(2)}) copy-start(s32[8,27]{1,0:T(8,128)} %param.18) | copy-start | bytes 2596
  633.8 14.7 %copy-start = (pred[512,2816]{1,0:T(8,128)(4,1)S(1)}, pred[512,2816]{1,0:T(8,128)(4,1)}, u32[]{:S(2)}) copy-start(pred[512,2816]{1,0:T(8,128)(4,1)} %copy.74) | copy-start | bytes 4325380 | tf_op jit(solution)/shard_map/while
  648.5 13.8 %copy-start.4 = (bf16[512,5,128]{0,2,1:T(8,128)(2,1)S(1)}, bf16[512,5,128]{0,2,1:T(8,128)(2,1)}, u32[]{:S(2)}) copy-start(bf16[512,5,128]{0,2,1:T(8,128)(2,1)} %get-tuple-element.318) | copy-start | bytes 1966084 | tf_op jit(solution)/shard_map/while
  695.8 14.7 %copy-start = (pred[512,2816]{1,0:T(8,128)(4,1)S(1)}, pred[512,2816]{1,0:T(8,128)(4,1)}, u32[]{:S(2)}) copy-start(pred[512,2816]{1,0:T(8,128)(4,1)} %copy.74) | copy-start | bytes 4325380 | tf_op jit(solution)/shard_map/while
  710.5 13.8 %copy-start.4 = (bf16[512,5,128]{0,2,1:T(8,128)(2,1)S(1)}, bf16[512,5,128]{0,2,1:T(8,128)(2,1)}, u32[]{:S(2)}) copy-start(bf16[512,5,128]{0,2,1:T(8,128)(2,1)} %get-tuple-element.318) | copy-start | bytes 1966084 | tf_op jit(solution)/shard_map/while
